TPU v7x, 256 devices: a whole 4x4x8 slice. The times are simulated.
256 devices in a mesh: gx: 64 (over z, y, x_hi), gy: 4 (over x_lo, core).
Axes of the slice: x: 4 (x_hi: 2, x_lo: 2; x = x_hi * 2 + x_lo), y: 4, z: 8, core: 2. Of those that a mesh axis runs over, the one named last changes fastest.
Arguments:
- pressure: float32 [256, 256, 128], P('gx', 'gy'), may hold values from 0.5 to 2
- sat_water: float32 [256, 256, 128], P('gx', 'gy'), may hold values from 0.15 to 0.45
- sat_gas: float32 [256, 256, 128], P('gx', 'gy'), may hold values from 0.05 to 0.35
- pore_volume: float32 [256, 256, 128], P('gx', 'gy'), may hold values from 0.05 to 0.5
- mass_old: float32 [3, 256, 256, 128], P(None, 'gx', 'gy'), may hold values from -1.5 to 1.5
- transmissibility: float32 [3, 256, 256, 128], P(None, 'gx', 'gy'), may hold values from 0.1 to 3
- upwind: int32 [3, 3, 256, 256, 128], P(None, None, 'gx', 'gy'), may hold values from 0 to 1
Outputs:
- residual: float32 [3, 256, 256, 128], P(None, 'gx', 'gy')
- diag_block: float32 [9, 256, 256, 128], P(None, 'gx', 'gy')
- lower_block: float32 [3, 9, 256, 256, 128], P(None, None, 'gx', 'gy')
- upper_block: float32 [3, 9, 256, 256, 128], P(None, None, 'gx', 'gy')
- pressure_rows: float32 [7, 256, 256, 128], P(None, 'gx', 'gy')
- prolongator: float32 [7, 256, 256, 128], P(None, 'gx', 'gy')
- coarse_rhs: float32 [128, 128, 128], P('gx', 'gy')
All inputs are finite; a program needn't handle non-finite values.
Results may differ from a plain program's by a relative error of at most 0.0001.
Values sent between devices are 32-bit elements; how exact they have to be, the bound alone decides.
No kernel may reach another device: no remote copies, remote signals or barrier semaphores. Data moves between devices by JAX's collectives and lax.ppermute only.
A program may use at most 64 MiB of HBM per device.

v0:
```python
import jax
import jax.numpy as jnp
from jax import lax
from jax.sharding import PartitionSpec as P

comp_water = 0.05
comp_oil = 0.1
rock_comp = 0.02
gas_ratio = 0.3
visc_water = 0.5
visc_oil = 2.0
visc_gas = 0.2
head_flat = (0.0, 0.0, 0.0)
head_depth = (0.1, 0.08, 0.02)
time_step = 0.5
damping = 2.0 / 3.0


def passed_along(value, axis, steps):
    count = lax.axis_size(axis)
    first, last = (max(0, -steps), min(count, count - steps))
    return lax.ppermute(value, axis, [(source, source + steps) for source in range(first, last)])


def with_halo(value, sides, width):
    edges = {}
    for axis, dim in sides:
        size, length = (lax.axis_size(axis), value.shape[dim])
        up = [(i, (i + 1) % size) for i in range(size - 1)]
        last = lax.slice_in_dim(value, length - width, length, axis=dim)
        first = lax.slice_in_dim(value, 0, width, axis=dim)
        edges[dim] = (
            lax.ppermute(last, axis, up),
            lax.ppermute(first, axis, [(b, a) for a, b in up]),
        )
    done = []
    for _, dim in sides:
        low, high = edges[dim]
        around = [(width, width) if d in done else (0, 0) for d in range(value.ndim)]
        value = jnp.concatenate([jnp.pad(low, around), value, jnp.pad(high, around)], axis=dim)
        done.append(dim)
    return value


def volumes(states):
    press = states[0]
    water = states[1]
    gas_sat = states[2]
    oil_sat = 1.0 - water - gas_sat
    b_water = 1.0 + comp_water * press
    b_oil = 1.0 + comp_oil * press
    return (press, water, gas_sat, oil_sat, b_water, b_oil, press)


def mobility(states):
    press, water, gas_sat, oil_sat, b_water, b_oil, b_gas = volumes(states)
    moving = jnp.stack(
        [
            water * water * b_water / visc_water,
            oil_sat * oil_sat * b_oil / visc_oil,
            gas_sat * gas_sat * b_gas / visc_gas,
        ]
    )
    return (moving, gas_ratio * press)


def face_flux(lower_state, upper_state, trans, upwind, head):
    mob_lower, solved_lower = mobility(lower_state)
    mob_upper, solved_upper = mobility(upper_state)
    chosen = upwind * mob_lower + (1.0 - upwind) * mob_upper
    drop = lower_state[0] - upper_state[0]
    heads = jnp.array(head, jnp.float32).reshape(3, 1, 1, 1)
    phases = trans[None] * chosen * (drop[None] + heads)
    solved = upwind[1] * solved_lower + (1.0 - upwind[1]) * solved_upper
    return jnp.stack([phases[0], phases[1], phases[2] + solved * phases[1]])


def unit_rows(template):
    return [
        jnp.stack(
            [
                jnp.ones_like(template[0]) if column == row else jnp.zeros_like(template[0])
                for column in range(3)
            ]
        )
        for row in range(3)
    ]


def face_terms(lower_state, upper_state, trans, upwind, head):
    fluxes, pullback = jax.vjp(
        lambda first, second: face_flux(first, second, trans, upwind, head),
        lower_state,
        upper_state,
    )
    by_lower = []
    by_upper = []
    for cotangent in unit_rows(fluxes):
        wrt_lower, wrt_upper = pullback(cotangent)
        by_lower.append(wrt_lower)
        by_upper.append(wrt_upper)
    return (fluxes, jnp.concatenate(by_lower, 0), jnp.concatenate(by_upper, 0))


def accumulate(states, pore_volume):
    press, water, gas_sat, oil_sat, b_water, b_oil, b_gas = volumes(states)
    porosity = pore_volume * (1.0 + rock_comp * press)
    return jnp.stack(
        [
            porosity * b_water * water,
            porosity * b_oil * oil_sat,
            porosity * (b_gas * gas_sat + gas_ratio * press * b_oil * oil_sat),
        ]
    )


def accumulation_terms(states, pore_volume):
    masses, pullback = jax.vjp(lambda first: accumulate(first, pore_volume), states)
    rows = [pullback(cotangent)[0] for cotangent in unit_rows(masses)]
    return (masses, jnp.concatenate(rows, 0))


def impes_weights(states):
    press, water, gas_sat, oil_sat, b_water, b_oil, b_gas = volumes(states)
    return jnp.stack([1.0 / b_water, 1.0 / b_oil - gas_ratio, 1.0 / b_gas])


def cut_layer(field, dimension, first_index, last_index):
    return lax.slice_in_dim(field, first_index, last_index, axis=dimension)


def raise_up(field, upper_face, dimension):
    count = field.shape[dimension]
    return jnp.concatenate([cut_layer(field, dimension, 1, count), upper_face], dimension)


def sink_down(field, lower_face, dimension):
    count = field.shape[dimension]
    return jnp.concatenate([lower_face, cut_layer(field, dimension, 0, count - 1)], dimension)


def face_field(states, below, dimension, start, trans, upwind, head):
    lower_state = sink_down(states, below, dimension)
    positions = start + lax.broadcasted_iota(jnp.int32, trans.shape, dimension - 1)
    trans_live = jnp.where(positions > 0, trans, jnp.zeros_like(trans))
    return face_terms(lower_state, states, trans_live, upwind, head)


def assemble(masses, acc_block, mass_old, faces_all, tops_all):
    residual = (masses - mass_old) / time_step
    diagonal = acc_block / time_step
    lowers = []
    uppers = []
    for direction in range(3):
        fluxes, by_lower, by_upper = faces_all[direction]
        flux_top, lower_top, upper_top = tops_all[direction]
        dimension = direction + 1
        residual = residual - fluxes + raise_up(fluxes, flux_top, dimension)
        diagonal = diagonal - by_upper + raise_up(by_lower, lower_top, dimension)
        lowers.append(-by_lower)
        uppers.append(raise_up(by_upper, upper_top, dimension))
    return (residual, diagonal, lowers, uppers)


def pressure_section(weight, acc_block, diagonal, lowers, uppers, odd_x, odd_y):

    def column(block):
        return jnp.sum(weight * block[0::3], axis=0)

    press_diag = column(diagonal)
    press_lower = [column(block) for block in lowers]
    press_upper = [column(block) for block in uppers]
    accum = column(acc_block) / time_step
    divisor = jnp.abs(press_diag) + accum
    for entry in press_lower + press_upper:
        divisor = divisor + jnp.abs(entry)
    scale = damping / divisor
    nothing = jnp.zeros_like(odd_x)
    same_lower = [odd_x, odd_y, nothing]
    same_upper = [1.0 - odd_x, 1.0 - odd_y, nothing]
    inside = press_diag
    for direction in range(3):
        inside = (
            inside
            + same_lower[direction] * press_lower[direction]
            + same_upper[direction] * press_upper[direction]
        )
    own_weight = 1.0 - scale * inside
    near_lower = [
        -scale * press_lower[direction] * (1.0 - same_lower[direction]) for direction in range(3)
    ]
    near_upper = [
        -scale * press_upper[direction] * (1.0 - same_upper[direction]) for direction in range(3)
    ]
    rows_out = jnp.stack([press_diag] + press_lower + press_upper)
    prolong = jnp.stack([own_weight] + near_lower + near_upper)
    return (rows_out, prolong)


def contributions(prolong, residual, weight):
    reduced = jnp.sum(weight * residual, axis=0)
    shares = prolong * reduced[None]
    layer_z = jnp.zeros_like(reduced[:, :, 0:1])
    local_sum = shares[0] + raise_up(shares[3], layer_z, 2) + sink_down(shares[6], layer_z, 2)
    sideways = jnp.stack([shares[1], shares[4], shares[2], shares[5]])
    return (local_sum, sideways)


def block_sum(field):
    span_a, span_b, span_c = field.shape[-3:]
    shaped = field.reshape(field.shape[:-3] + (span_a // 2, 2, span_b // 2, 2, span_c))
    return jnp.sum(shaped, axis=(-4, -2))


def split_terms(received):
    return (received[0:3], received[3:12], received[12:21])


def body(pressure, sat_water, sat_gas, pore_volume, mass_old, transmissibility, upwind):
    span_x, span_y, depth = pressure.shape
    states = jnp.stack([pressure, sat_water, sat_gas])
    masses, acc_block = accumulation_terms(states, pore_volume)
    weight = impes_weights(states)
    flags = upwind.astype(jnp.float32)
    below_x = passed_along(cut_layer(states, 1, span_x - 1, span_x), "gx", 1)
    below_y = passed_along(cut_layer(states, 2, span_y - 1, span_y), "gy", 1)
    start_x = lax.axis_index("gx") * span_x
    start_y = lax.axis_index("gy") * span_y
    faces_x = face_field(states, below_x, 1, start_x, transmissibility[0], flags[0], head_flat)
    faces_y = face_field(states, below_y, 2, start_y, transmissibility[1], flags[1], head_flat)
    below_z = jnp.zeros_like(cut_layer(states, 3, 0, 1))
    faces_z = face_field(states, below_z, 3, 0, transmissibility[2], flags[2], head_depth)
    packed_x = jnp.concatenate([cut_layer(part, 1, 0, 1) for part in faces_x], 0)
    top_x = split_terms(passed_along(packed_x, "gx", -1))
    packed_y = jnp.concatenate([cut_layer(part, 2, 0, 1) for part in faces_y], 0)
    top_y = split_terms(passed_along(packed_y, "gy", -1))
    zero_nine = jnp.zeros_like(cut_layer(acc_block, 3, 0, 1))
    top_z = (below_z, zero_nine, zero_nine)
    residual, diagonal, lowers, uppers = assemble(
        masses, acc_block, mass_old, [faces_x, faces_y, faces_z], [top_x, top_y, top_z]
    )
    odd_x = (lax.broadcasted_iota(jnp.int32, pressure.shape, 0) % 2).astype(jnp.float32)
    odd_y = (lax.broadcasted_iota(jnp.int32, pressure.shape, 1) % 2).astype(jnp.float32)
    rows_out, prolong = pressure_section(weight, acc_block, diagonal, lowers, uppers, odd_x, odd_y)
    local_sum, sideways = contributions(prolong, residual, weight)
    wider = with_halo(sideways, (("gx", 1), ("gy", 2)), 1)
    total = (
        local_sum
        + wider[0, 2:, 1:-1]
        + wider[1, :-2, 1:-1]
        + wider[2, 1:-1, 2:]
        + wider[3, 1:-1, :-2]
    )
    coarse = block_sum(total)
    return (residual, diagonal, jnp.stack(lowers), jnp.stack(uppers), rows_out, prolong, coarse)


def solution(mesh):
    in_specs = (
        P("gx", "gy", None),
        P("gx", "gy", None),
        P("gx", "gy", None),
        P("gx", "gy", None),
        P(None, "gx", "gy", None),
        P(None, "gx", "gy", None),
        P(None, None, "gx", "gy", None),
    )
    out_specs = (
        P(None, "gx", "gy", None),
        P(None, "gx", "gy", None),
        P(None, None, "gx", "gy", None),
        P(None, None, "gx", "gy", None),
        P(None, "gx", "gy", None),
        P(None, "gx", "gy", None),
        P("gx", "gy", None),
    )
    return jax.shard_map(body, mesh=mesh, in_specs=in_specs, out_specs=out_specs, check_vma=False)
```

profile of v0, /device:TPU:129, one launch (start us, length us, event | category | flops | bytes accessed | tf_op | source)
XLA Modules:
  0.0 80.2 jit_solution(18248587491792656176)
XLA Ops:
  0.6 1.1 %pad_maximum_fusion.16 = f32[3,4,64,128]{3,2,1,0:T(8,128)S(1)} fusion(f32[1,4,64,128]{3,2,1,0:T(8,128)} %bitcast.776, f32[1,4,64,128]{3,2,1,0:T(8,128)} %bitcast.774, f32[1,4,64,128]{3,2,1,0:T(8,128)} %bitcast.778), kind=kLoop, calls=%fused_computation.89 | loop fusion | flops 196608 | bytes 786432 | tf_op jit(solution)/shard_map/stack | solution.py:221
  1.8 4.8 %collective-permute-start = (f32[3,1,64,128]{3,2,1,0:T(8,128)S(1)}, f32[3,1,64,128]{3,2,1,0:T(8,128)S(1)}, u32[]{:S(2)}, u32[]{:S(2)}) collective-permute-start(f32[3,1,64,128]{3,2,1,0:T(8,128)S(1)} %slice.335), channel_id=1, source_target_pairs={{0,4},{4,8},{8,12},{12,16},{16,20},{20,24},{24,28},{28,32},{32,36}... | collective-permute-start | bytes 294920 | tf_op jit(solution)/shard_map/ppermute | solution.py:22
  6.6 0.8 pad_maximum_fusion.42
  7.3 3.0 %collective-permute-start.2 = (f32[3,4,1,128]{3,2,1,0:T(1,128)S(1)}, f32[3,4,1,128]{3,2,1,0:T(1,128)S(1)}, u32[]{:S(2)}, u32[]{:S(2)}) collective-permute-start(f32[3,4,1,128]{3,2,1,0:T(1,128)S(1)} %pad_maximum_fusion.42), channel_id=1, source_target_pairs={{0,1},{1,2},{2,3},{4,5},{5,6},{6,7},{8,9},{9,10},{10,11},{12,13},{... | collective-permute-start | bytes 18440 | tf_op jit(solution)/shard_map/ppermute | solution.py:22
  11.1 1.9 %collective-permute-done = f32[3,1,64,128]{3,2,1,0:T(8,128)S(1)} collective-permute-done((f32[3,1,64,128]{3,2,1,0:T(8,128)S(1)}, f32[3,1,64,128]{3,2,1,0:T(8,128)S(1)}, u32[]{:S(2)}, u32[]{:S(2)}) %collective-permute-start) | collective-permute-done | bytes 98336 | tf_op jit(solution)/shard_map/ppermute | solution.py:22
  14.5 0.7 copy-done
  15.6 0.8 multiply_add_fusion.5
  22.1 3.7 %collective-permute-start.3 = (f32[21,4,1,128]{3,2,1,0:T(1,128)S(1)}, f32[21,4,1,128]{3,2,1,0:T(1,128)S(1)}, u32[]{:S(2)}, u32[]{:S(2)}) collective-permute-start(f32[21,4,1,128]{3,2,1,0:T(1,128)S(1)} %pad_maximum_fusion.39), channel_id=1, source_target_pairs={{1,0},{2,1},{3,2},{5,4},{6,5},{7,6},{9,8},{10,9},{11,10},{13,12},{... | collective-permute-start | bytes 129032 | tf_op jit(solution)/shard_map/ppermute | solution.py:22
  26.4 0.7 copy-done.3
  27.2 0.9 %slice-done = f32[9,1,64,128]{3,2,1,0:T(8,128)S(1)} async-done(((f32[9,4,64,128]{3,2,1,0:T(8,128)}), f32[9,1,64,128]{3,2,1,0:T(8,128)S(1)}, s32[]{:S(2)}) %slice-start) | async-done | bytes 294936 | tf_op jit(solution)/shard_map/slice | solution.py:129
  28.2 5.0 %collective-permute-start.1 = (f32[21,1,64,128]{3,2,1,0:T(8,128)S(1)}, f32[21,1,64,128]{3,2,1,0:T(8,128)S(1)}, u32[]{:S(2)}, u32[]{:S(2)}) collective-permute-start(f32[21,1,64,128]{3,2,1,0:T(8,128)S(1)} %pad_maximum_fusion.11), channel_id=1, source_target_pairs={{4,0},{8,4},{12,8},{16,12},{20,16},{24,20},{28,24},{32,28},{36,32}... | collective-permute-start | bytes 2064392 | tf_op jit(solution)/shard_map/ppermute | solution.py:22
  34.7 2.0 %pad_maximum_fusion = f32[3,9,4,64,128]{4,3,2,1,0:T(8,128)} fusion(f32[1,9,4,64,128]{4,3,2,1,0:T(8,128)S(1)} %maximum_negate_fusion.2, f32[1,9,4,64,128]{4,3,2,1,0:T(8,128)S(1)} %maximum_negate_fusion.1, f32[1,9,4,64,128]{4,3,2,1,0:T(8,128)S(1)} %maximum_negate_fusion), kind=kLoop, calls=%fused_computation | loop fusion | flops 1769472 | bytes 7077888 | tf_op jit(solution)/shard_map/stack | solution.py:255
  38.7 10.0 %collective-permute-done.1 = f32[21,1,64,128]{3,2,1,0:T(8,128)S(1)} collective-permute-done((f32[21,1,64,128]{3,2,1,0:T(8,128)S(1)}, f32[21,1,64,128]{3,2,1,0:T(8,128)S(1)}, u32[]{:S(2)}, u32[]{:S(2)}) %collective-permute-start.1) | collective-permute-done | bytes 688160 | tf_op jit(solution)/shard_map/ppermute | solution.py:22
  49.0 1.0 %fusion.3 = f32[9,4,64,128]{3,2,1,0:T(8,128)S(1)} fusion(f32[9,1,64,128]{3,2,1,0:T(8,128)S(1)} %get-tuple-element.133, f32[9,3,64,128]{3,2,1,0:T(8,128)S(1)} %slice.377, f32[9,4,1,128]{3,2,1,0:T(1,128)S(1)} %get-tuple-element.224, f32[9,4,63,128]{3,2,1,0:T(8,128)S(1)} %slice.379, f32[9,4,64,127]{3,2,1,0:T(8,128)S(1)} %slice.381, ...), kind=kLoop, calls=%fused_computation.23 | loop fusion | flops 5013504 | bytes 9427968 | tf_op jit(solution)/shard_map/add | solution.py:159
  51.3 1.3 %multiply_reduce_fusion = (f32[4,64,128]{2,1,0:T(8,128)S(1)}, f32[4,64,128]{2,1,0:T(8,128)S(1)}, f32[4,64,128]{2,1,0:T(8,128)S(1)}, f32[4,64,128]{2,1,0:T(8,128)S(1)}, f32[3,4,64,128]{3,2,1,0:T(8,128)}) fusion(f32[1,4,64,128]{3,2,1,0:T(8,128)S(1)} %get-tuple-element.221, f32[1,4,64,128]{3,2,1,0:T(8,128)S(1)} %get-tuple-element.220, ...), kind=kLoop, calls=%fused_computation.101 | loop fusion | flops 2326528 | bytes 5633024 | tf_op jit(solution)/shard_map/reduce_sum | solution.py:201
  53.5 0.7 copy-done.5
  54.6 3.7 %collective-permute-start.7 = (f32[4,4,1,128]{3,2,1,0:T(1,128)S(1)}, f32[4,4,1,128]{3,2,1,0:T(1,128)S(1)}, u32[]{:S(2)}, u32[]{:S(2)}) collective-permute-start(f32[4,4,1,128]{3,2,1,0:T(1,128)S(1)} %get-tuple-element.135), channel_id=1, source_target_pairs={{0,1},{1,2},{2,3},{4,5},{5,6},{6,7},{8,9},{9,10},{10,11},{12,13},{... | collective-permute-start | bytes 24584 | tf_op jit(solution)/shard_map/ppermute | solution.py:33
  58.3 9.6 %collective-permute-start.4 = (f32[4,1,64,128]{3,2,1,0:T(8,128)S(1)}, f32[4,1,64,128]{3,2,1,0:T(8,128)S(1)}, u32[]{:S(2)}, u32[]{:S(2)}) collective-permute-start(f32[4,1,64,128]{3,2,1,0:T(8,128)S(1)} %get-tuple-element.137), channel_id=1, source_target_pairs={{4,0},{8,4},{12,8},{16,12},{20,16},{24,20},{28,24},{32,28},{36,32}... | collective-permute-start | bytes 393224 | tf_op jit(solution)/shard_map/ppermute | solution.py:34
  67.9 1.9 %collective-permute-start.5 = (f32[4,1,64,128]{3,2,1,0:T(8,128)S(1)}, f32[4,1,64,128]{3,2,1,0:T(8,128)S(1)}, u32[]{:S(2)}, u32[]{:S(2)}) collective-permute-start(f32[4,1,64,128]{3,2,1,0:T(8,128)S(1)} %get-tuple-element.136), channel_id=1, source_target_pairs={{0,4},{4,8},{8,12},{12,16},{16,20},{20,24},{24,28},{28,32},{32,36}... | collective-permute-start | bytes 393224 | tf_op jit(solution)/shard_map/ppermute | solution.py:33
  69.9 1.9 %collective-permute-start.6 = (f32[4,4,1,128]{3,2,1,0:T(1,128)S(1)}, f32[4,4,1,128]{3,2,1,0:T(1,128)S(1)}, u32[]{:S(2)}, u32[]{:S(2)}) collective-permute-start(f32[4,4,1,128]{3,2,1,0:T(1,128)S(1)} %get-tuple-element.134), channel_id=1, source_target_pairs={{1,0},{2,1},{3,2},{5,4},{6,5},{7,6},{9,8},{10,9},{11,10},{13,12},{... | collective-permute-start | bytes 24584 | tf_op jit(solution)/shard_map/ppermute | solution.py:34
  71.8 2.0 %pad_maximum_fusion.1 = f32[3,9,4,64,128]{4,3,2,1,0:T(8,128)} fusion(f32[1,9,4,64,128]{4,3,2,1,0:T(8,128)S(1)} %pad_bitcast_fusion, f32[1,9,4,64,128]{4,3,2,1,0:T(8,128)S(1)} %fusion.192, f32[1,9,4,64,128]{4,3,2,1,0:T(8,128)S(1)} %get-tuple-element.87), kind=kLoop, calls=%fused_computation.1 | loop fusion | flops 1769472 | bytes 7077888 | tf_op jit(solution)/shard_map/stack | solution.py:255
  73.9 1.2 %collective-permute-done.6 = f32[4,4,1,128]{3,2,1,0:T(1,128)S(1)} collective-permute-done((f32[4,4,1,128]{3,2,1,0:T(1,128)S(1)}, f32[4,4,1,128]{3,2,1,0:T(1,128)S(1)}, u32[]{:S(2)}, u32[]{:S(2)}) %collective-permute-start.6) | collective-permute-done | bytes 8224 | tf_op jit(solution)/shard_map/ppermute | solution.py:34
  75.1 4.2 %collective-permute-done.5 = f32[4,1,64,128]{3,2,1,0:T(8,128)S(1)} collective-permute-done((f32[4,1,64,128]{3,2,1,0:T(8,128)S(1)}, f32[4,1,64,128]{3,2,1,0:T(8,128)S(1)}, u32[]{:S(2)}, u32[]{:S(2)}) %collective-permute-start.5) | collective-permute-done | bytes 131104 | tf_op jit(solution)/shard_map/ppermute | solution.py:33
  79.5 0.7 reduce_sum.234
  (158 shorter events, 14.7 us)
Async XLA Ops:
  0.6 10.1 %copy-start.8 = (f32[3,4,64,128]{3,2,1,0:T(8,128)S(1)}, f32[3,4,64,128]{3,2,1,0:T(8,128)}, u32[]{:S(2)}) copy-start(f32[3,4,64,128]{3,2,1,0:T(8,128)} %param.15) | copy-start | bytes 1179652
  1.8 9.1 %copy-start.6 = (s32[3,3,4,64,128]{4,3,2,1,0:T(8,128)S(1)}, s32[3,3,4,64,128]{4,3,2,1,0:T(8,128)}, u32[]{:S(2)}) copy-start(s32[3,3,4,64,128]{4,3,2,1,0:T(8,128)} %param.16) | copy-start | bytes 3538948
  1.8 11.2 %collective-permute-start = (f32[3,1,64,128]{3,2,1,0:T(8,128)S(1)}, f32[3,1,64,128]{3,2,1,0:T(8,128)S(1)}, u32[]{:S(2)}, u32[]{:S(2)}) collective-permute-start(f32[3,1,64,128]{3,2,1,0:T(8,128)S(1)} %slice.335), channel_id=1, source_target_pairs={{0,4},{4,8},{8,12},{12,16},{16,20},{20,24},{24,28},{28,32},{32,36}... | collective-permute-start | bytes 294920 | tf_op jit(solution)/shard_map/ppermute | solution.py:22
  7.3 3.8 %collective-permute-start.2 = (f32[3,4,1,128]{3,2,1,0:T(1,128)S(1)}, f32[3,4,1,128]{3,2,1,0:T(1,128)S(1)}, u32[]{:S(2)}, u32[]{:S(2)}) collective-permute-start(f32[3,4,1,128]{3,2,1,0:T(1,128)S(1)} %pad_maximum_fusion.42), channel_id=1, source_target_pairs={{0,1},{1,2},{2,3},{4,5},{5,6},{6,7},{8,9},{9,10},{10,11},{12,13},{... | collective-permute-start | bytes 18440 | tf_op jit(solution)/shard_map/ppermute | solution.py:22
  10.8 2.2 %copy-start.2 = (f32[4,64,128]{2,1,0:T(8,128)S(1)}, f32[4,64,128]{2,1,0:T(8,128)}, u32[]{:S(2)}) copy-start(f32[4,64,128]{2,1,0:T(8,128)} %param.10) | copy-start | bytes 393220
  13.0 0.7 copy-start.12
  14.3 0.9 %copy-start = (f32[4,64,128]{2,1,0:T(8,128)S(1)}, f32[4,64,128]{2,1,0:T(8,128)}, u32[]{:S(2)}) copy-start(f32[4,64,128]{2,1,0:T(8,128)} %param.11) | copy-start | bytes 393220
  14.3 1.0 %copy-start.1 = (f32[4,64,128]{2,1,0:T(8,128)S(1)}, f32[4,64,128]{2,1,0:T(8,128)}, u32[]{:S(2)}) copy-start(f32[4,64,128]{2,1,0:T(8,128)} %param.12) | copy-start | bytes 393220
  15.6 0.9 %copy-start.9 = (f32[4,64,128]{2,1,0:T(8,128)S(1)}, f32[4,64,128]{2,1,0:T(8,128)}, u32[]{:S(2)}) copy-start(f32[4,64,128]{2,1,0:T(8,128)} %param.13) | copy-start | bytes 393220
  22.1 15.8 %collective-permute-start.3 = (f32[21,4,1,128]{3,2,1,0:T(1,128)S(1)}, f32[21,4,1,128]{3,2,1,0:T(1,128)S(1)}, u32[]{:S(2)}, u32[]{:S(2)}) collective-permute-start(f32[21,4,1,128]{3,2,1,0:T(1,128)S(1)} %pad_maximum_fusion.39), channel_id=1, source_target_pairs={{1,0},{2,1},{3,2},{5,4},{6,5},{7,6},{9,8},{10,9},{11,10},{13,12},{... | collective-permute-start | bytes 129032 | tf_op jit(solution)/shard_map/ppermute | solution.py:22
  26.1 1.0 %copy-start.3 = (f32[9,4,64,128]{3,2,1,0:T(8,128)}, f32[9,4,64,128]{3,2,1,0:T(8,128)S(1)}, u32[]{:S(2)}) copy-start(f32[9,4,64,128]{3,2,1,0:T(8,128)S(1)} %pad_maximum_fusion.3) | copy-start | bytes 3538948
  27.1 1.0 %slice-start = ((f32[9,4,64,128]{3,2,1,0:T(8,128)}), f32[9,1,64,128]{3,2,1,0:T(8,128)S(1)}, s32[]{:S(2)}) async-start(f32[9,4,64,128]{3,2,1,0:T(8,128)} %copy-done.3), calls=%async_computation | async-start | bytes 589824 | tf_op jit(solution)/shard_map/slice | solution.py:129
  28.2 20.5 %collective-permute-start.1 = (f32[21,1,64,128]{3,2,1,0:T(8,128)S(1)}, f32[21,1,64,128]{3,2,1,0:T(8,128)S(1)}, u32[]{:S(2)}, u32[]{:S(2)}) collective-permute-start(f32[21,1,64,128]{3,2,1,0:T(8,128)S(1)} %pad_maximum_fusion.11), channel_id=1, source_target_pairs={{4,0},{8,4},{12,8},{16,12},{20,16},{24,20},{28,24},{32,28},{36,32}... | collective-permute-start | bytes 2064392 | tf_op jit(solution)/shard_map/ppermute | solution.py:22
  37.9 0.6 copy-start.10
  38.6 10.1 %slice-start.1 = ((f32[9,4,64,128]{3,2,1,0:T(8,128)}), f32[9,3,64,128]{3,2,1,0:T(8,128)S(1)}, s32[]{:S(2)}) async-start(f32[9,4,64,128]{3,2,1,0:T(8,128)} %copy-done.3), calls=%async_computation.1 | async-start | bytes 1769472 | tf_op jit(solution)/shard_map/slice | solution.py:129
  50.0 1.0 %copy-start.4 = (f32[9,4,64,128]{3,2,1,0:T(8,128)}, f32[9,4,64,128]{3,2,1,0:T(8,128)S(1)}, u32[]{:S(2)}) copy-start(f32[9,4,64,128]{3,2,1,0:T(8,128)S(1)} %fusion.3) | copy-start | bytes 3538948
  50.0 1.3 %copy-start.7 = (f32[3,4,64,128]{3,2,1,0:T(8,128)S(1)}, f32[3,4,64,128]{3,2,1,0:T(8,128)}, u32[]{:S(2)}) copy-start(f32[3,4,64,128]{3,2,1,0:T(8,128)} %param.14) | copy-start | bytes 1179652
  50.0 1.3 %slice-start.2 = ((f32[21,4,1,128]{3,2,1,0:T(1,128)}), f32[3,4,1,128]{3,2,1,0:T(1,128)S(1)}, s32[]{:S(2)}) async-start(f32[21,4,1,128]{3,2,1,0:T(1,128)} %copy-done.10), calls=%async_computation.2 | async-start | bytes 12288 | tf_op jit(solution)/shard_map/slice | solution.py:216
  53.3 0.9 %copy-start.5 = (f32[7,4,64,128]{3,2,1,0:T(8,128)}, f32[7,4,64,128]{3,2,1,0:T(8,128)S(1)}, u32[]{:S(2)}) copy-start(f32[7,4,64,128]{3,2,1,0:T(8,128)S(1)} %get-tuple-element.206) | copy-start | bytes 2752516
  53.3 1.2 %copy-start.11 = (f32[7,4,64,128]{3,2,1,0:T(8,128)}, f32[7,4,64,128]{3,2,1,0:T(8,128)S(1)}, u32[]{:S(2)}) copy-start(f32[7,4,64,128]{3,2,1,0:T(8,128)S(1)} %get-tuple-element.207) | copy-start | bytes 2752516
  54.6 19.4 %collective-permute-start.7 = (f32[4,4,1,128]{3,2,1,0:T(1,128)S(1)}, f32[4,4,1,128]{3,2,1,0:T(1,128)S(1)}, u32[]{:S(2)}, u32[]{:S(2)}) collective-permute-start(f32[4,4,1,128]{3,2,1,0:T(1,128)S(1)} %get-tuple-element.135), channel_id=1, source_target_pairs={{0,1},{1,2},{2,3},{4,5},{5,6},{6,7},{8,9},{9,10},{10,11},{12,13},{... | collective-permute-start | bytes 24584 | tf_op jit(solution)/shard_map/ppermute | solution.py:33
  58.3 16.8 %collective-permute-start.4 = (f32[4,1,64,128]{3,2,1,0:T(8,128)S(1)}, f32[4,1,64,128]{3,2,1,0:T(8,128)S(1)}, u32[]{:S(2)}, u32[]{:S(2)}) collective-permute-start(f32[4,1,64,128]{3,2,1,0:T(8,128)S(1)} %get-tuple-element.137), channel_id=1, source_target_pairs={{4,0},{8,4},{12,8},{16,12},{20,16},{24,20},{28,24},{32,28},{36,32}... | collective-permute-start | bytes 393224 | tf_op jit(solution)/shard_map/ppermute | solution.py:34
  67.9 11.4 %collective-permute-start.5 = (f32[4,1,64,128]{3,2,1,0:T(8,128)S(1)}, f32[4,1,64,128]{3,2,1,0:T(8,128)S(1)}, u32[]{:S(2)}, u32[]{:S(2)}) collective-permute-start(f32[4,1,64,128]{3,2,1,0:T(8,128)S(1)} %get-tuple-element.136), channel_id=1, source_target_pairs={{0,4},{4,8},{8,12},{12,16},{16,20},{20,24},{24,28},{28,32},{32,36}... | collective-permute-start | bytes 393224 | tf_op jit(solution)/shard_map/ppermute | solution.py:33
  69.9 5.3 %collective-permute-start.6 = (f32[4,4,1,128]{3,2,1,0:T(1,128)S(1)}, f32[4,4,1,128]{3,2,1,0:T(1,128)S(1)}, u32[]{:S(2)}, u32[]{:S(2)}) collective-permute-start(f32[4,4,1,128]{3,2,1,0:T(1,128)S(1)} %get-tuple-element.134), channel_id=1, source_target_pairs={{1,0},{2,1},{3,2},{5,4},{6,5},{7,6},{9,8},{10,9},{11,10},{13,12},{... | collective-permute-start | bytes 24584 | tf_op jit(solution)/shard_map/ppermute | solution.py:34
where the time goes:
time: 80.7 us; the launch traced here: 80.2 us
  starting transfers between devices  33.7 us (42%)
  other arithmetic  20.3 us (25%)
  waiting for transfers between devices  17.5 us (22%)
  local copies, waits for them, and re-layouts  7.05 us (9%)
  between operations  1.68 us (2%)
    ppermute x4, starting transfers between devices, passed_along(): lax.ppermute(value, axis, [(source, source + steps) for source in range(f...  16.5 us
    ppermute x4, waiting for transfers between devices, passed_along(): lax.ppermute(value, axis, [(source, source + steps) for source in range(f...  12.1 us
    ppermute x2, starting transfers between devices, with_halo(): lax.ppermute(first, axis, [(b, a) for a, b in up])  11.5 us
    ppermute x2, starting transfers between devices, with_halo(): lax.ppermute(last, axis, up)  5.63 us
    unnamed x26, local copies, waits for them, and re-layouts  4.52 us
    ppermute x2, waiting for transfers between devices, with_halo(): lax.ppermute(last, axis, up)  4.24 us
    slice x15, local copies, waits for them, and re-layouts, cut_layer(): return lax.slice_in_dim(field, first_index, last_index, axis=dimension)  2.18 us
    another operation x2, other arithmetic, body(): jnp.stack(uppers)  2.15 us
  transfers between devices with their start and end apart: 8, of which 5 were waited for; matrix products, arithmetic and copies ran while one was open for 11% of the time, Pallas kernels for 0%

commit v1 on v0

v1 whole, which is shorter than its diff:
```python
import jax
import jax.numpy as jnp
from jax import lax
from jax.experimental import pallas as pl
from jax.experimental.pallas import tpu as pltpu
from jax.sharding import PartitionSpec as P

comp_water = 0.05
comp_oil = 0.1
rock_comp = 0.02
gas_ratio = 0.3
head_flat = (0.0, 0.0, 0.0)
head_depth = (0.1, 0.08, 0.02)
damping = 2.0 / 3.0
f32 = jnp.float32

distinct = 7
entry_of = (0, 1, -1, 2, 3, 3, 4, 5, 6)


def mobility_set(press, water, gas_sat):
    oil_sat = 1.0 - water - gas_sat
    b_water = 1.0 + comp_water * press
    b_oil = 1.0 + comp_oil * press
    water_sq = water * water
    oil_sq = oil_sat * oil_sat
    gas_sq = 5.0 * (gas_sat * gas_sat)
    return {
        "p": press,
        "rs": gas_ratio * press,
        "value": (2.0 * (water_sq * b_water), 0.5 * (oil_sq * b_oil), gas_sq * press),
        "by_p": ((2.0 * comp_water) * water_sq, (0.5 * comp_oil) * oil_sq, gas_sq),
        "by_s": (4.0 * (water * b_water), -(oil_sat * b_oil), 10.0 * (gas_sat * press)),
    }


def face(low, high, trans, flags, head):
    drop = low["p"] - high["p"]
    flux, lp, ls, hp, hs = [], [], [], [], []
    for a in range(3):
        push = trans * (drop + head[a]) if head[a] != 0.0 else trans * drop
        chosen = jnp.where(flags[a], low["value"][a], high["value"][a])
        moved = trans * chosen
        push_low = jnp.where(flags[a], push, 0.0)
        push_high = jnp.where(flags[a], 0.0, push)
        flux.append(push * chosen)
        lp.append(push_low * low["by_p"][a] + moved)
        hp.append(push_high * high["by_p"][a] - moved)
        ls.append(push_low * low["by_s"][a])
        hs.append(push_high * high["by_s"][a])
    solved = jnp.where(flags[1], low["rs"], high["rs"])
    extra = gas_ratio * flux[1]
    by_low = [
        lp[0], ls[0], lp[1], ls[1],
        lp[2] + solved * lp[1] + jnp.where(flags[1], extra, 0.0),
        solved * ls[1],
        ls[2] + solved * ls[1],
    ]
    by_high = [
        hp[0], hs[0], hp[1], hs[1],
        hp[2] + solved * hp[1] + jnp.where(flags[1], 0.0, extra),
        solved * hs[1],
        hs[2] + solved * hs[1],
    ]
    return [flux[0], flux[1], flux[2] + solved * flux[1]], by_low, by_high


def accumulation(press, water, gas_sat, pore):
    oil_sat = 1.0 - water - gas_sat
    b_water = 1.0 + comp_water * press
    b_oil = 1.0 + comp_oil * press
    porosity = pore * (1.0 + rock_comp * press)
    by_rock = rock_comp * pore
    in_water = b_water * water
    in_oil = b_oil * oil_sat
    solved = gas_ratio * press
    in_gas = press * gas_sat + solved * in_oil
    masses = [porosity * in_water, porosity * in_oil, porosity * in_gas]
    oil_by_s = -(porosity * b_oil)
    gas_by_water = solved * oil_by_s
    block = [
        by_rock * in_water + porosity * (comp_water * water),
        porosity * b_water,
        by_rock * in_oil + porosity * (comp_oil * oil_sat),
        oil_by_s,
        by_rock * in_gas
        + porosity * (gas_sat + gas_ratio * in_oil + (gas_ratio * comp_oil) * (press * oil_sat)),
        gas_by_water,
        porosity * press + gas_by_water,
    ]
    return masses, block


def weights_of(press):
    return (
        1.0 / (1.0 + comp_water * press),
        1.0 / (1.0 + comp_oil * press) - gas_ratio,
        1.0 / press,
    )


def column(weight, block):
    return weight[0] * block[0] + weight[1] * block[2] + weight[2] * block[4]


def prolong_of(cols, accum, x_odd, row_odd):
    divisor = jnp.abs(cols[0]) + accum
    for entry in cols[1:]:
        divisor = divisor + jnp.abs(entry)
    scale = damping / divisor
    same_x, far_x = (cols[1], cols[4]) if x_odd else (cols[4], cols[1])
    inside = cols[0] + same_x + jnp.where(row_odd, cols[2], cols[5])
    far_x = -scale * far_x
    nothing = jnp.zeros_like(far_x)
    return [
        1.0 - scale * inside,
        nothing if x_odd else far_x,
        jnp.where(row_odd, 0.0, -scale * cols[2]),
        -scale * cols[3],
        far_x if x_odd else nothing,
        jnp.where(row_odd, -scale * cols[5], 0.0),
        -scale * cols[6],
    ]


def shares_of(weights, reduced, lanes):
    near = weights[0] * reduced
    near = near + pltpu.roll(weights[3] * reduced, lanes - 1, 1)
    near = near + pltpu.roll(weights[6] * reduced, 1, 1)
    return near, (weights[2] + weights[5]) * reduced


def pack_kernel(p_hbm, w_hbm, g_hbm, t_hbm, u_hbm, xup, xdn, yev, yod, top, bot, bot_t, bot_u, face_u, sem):
    span_x, span_y, _ = p_hbm.shape
    rows = top.shape[2]
    copies = []

    def fetch(src, dst):
        copy = pltpu.make_async_copy(src, dst, sem.at[len(copies)])
        copy.start()
        copies.append(copy)

    for k, src in enumerate((p_hbm, w_hbm, g_hbm)):
        fetch(src.at[:, pl.ds(span_y - rows, rows)], top.at[k])
        fetch(src.at[:, pl.ds(0, rows)], bot.at[k])
    fetch(t_hbm.at[1, :, pl.ds(0, rows)], bot_t)
    fetch(u_hbm.at[1, :, :, pl.ds(0, rows)], bot_u)
    fetch(t_hbm.at[0, 0], xdn.at[3])
    fetch(u_hbm.at[0, :, 0], face_u)
    for k, src in enumerate((p_hbm, w_hbm, g_hbm)):
        fetch(src.at[span_x - 1], xup.at[k])
        fetch(src.at[0], xdn.at[k])
    for copy in copies:
        copy.wait()
    at_x0 = lax.axis_index("gx") == 0
    at_y0 = lax.axis_index("gy") == 0
    even = lax.axis_index("gy") % 2 == 0
    below = [bot[k, :, 0, :] for k in range(3)]
    below.append(jnp.where(at_y0, 0.0, bot_t[:, 0, :]))
    below += [bot_u[k, :, 0, :].astype(f32) for k in range(3)]
    above = [top[k, :, rows - 1, :] for k in range(3)]
    above += [jnp.zeros_like(above[0])] * 4
    for k in range(7):
        yev[k] = jnp.where(even, above[k], below[k])
        yod[k] = jnp.where(even, below[k], above[k])
    xdn[3] = jnp.where(at_x0, 0.0, xdn[3])
    for k in range(3):
        xdn[4 + k] = face_u[k].astype(f32)


def main_kernel(
    p_ref, w_ref, g_ref, v_ref, old_ref, t_ref, u_ref, yev, yod,
    res_hbm, diag_hbm, low_hbm, up_hbm, rows_hbm, pro_hbm, part, coarse, coarse_y,
    o_res, o_diag, o_low, o_up, o_rows, o_pro, fy, edge, sem,
):
    span_x, span_y, lanes = p_ref.shape
    size = 8
    chunks = span_y // size
    gy = lax.axis_index("gy")
    even = gy % 2 == 0
    row = lax.broadcasted_iota(jnp.int32, (size, lanes), 0)
    lane = lax.broadcasted_iota(jnp.int32, (size, lanes), 1)
    row_odd = row % 2 == 1
    first_row = row == 0
    zero = jnp.zeros((size, lanes), f32)
    last_x = span_x - 1

    def halo(k, upper):
        return jnp.where(even == upper, yev[k], yod[k])

    top = [jnp.concatenate([ref[x, span_y - 1 : span_y, :] for x in range(span_x)], 0) for ref in (p_ref, w_ref, g_ref)]
    above = [halo(k, True) for k in range(7)]
    flux, by_low, by_high = face(
        mobility_set(*top), mobility_set(*above[:3]), above[3], [a > 0.5 for a in above[4:]], head_flat
    )
    for x in range(span_x):
        for k, value in enumerate(flux + by_low + by_high):
            fy[x, k, size : size + 1, :] = value[x : x + 1]
    for k in range(3):
        edge[k] = halo(k, False)

    def chunk(step, carry):
        c = chunks - 1 - step
        base = pl.multiple_of(c * size, size)
        here = pl.ds(base, size)
        before = jnp.maximum(base - 1, 0)
        bottom = c == 0
        live_y = jnp.logical_or(jnp.logical_not(first_row), gy * span_y + base > 0)
        states = [(p_ref[x, here, :], w_ref[x, here, :], g_ref[x, here, :]) for x in range(1)]
        own_next = mobility_set(*states[0])
        state_next = states[0]
        x_face = None
        for x in range(span_x):
            own, state = own_next, state_next
            weight = weights_of(state[0])
            masses, acc = accumulation(*state, v_ref[x, here, :])
            res = [2.0 * (masses[k] - old_ref[k, x, here, :]) for k in range(3)]
            accum = 2.0 * column(weight, acc)
            diag = [2.0 * entry for entry in acc]
            cols = [None] * 7

            def put(ref, direction, block, sign):
                for k in range(9):
                    value = zero if entry_of[k] < 0 else block[entry_of[k]]
                    ref[direction, k, x, here, :] = -value if sign < 0 and entry_of[k] >= 0 else value

            if x_face is not None:
                flux, by_low, by_high = x_face
                res = [a - b for a, b in zip(res, flux)]
                diag = [a - b for a, b in zip(diag, by_high)]
                put(o_low, 0, by_low, -1)
                cols[1] = -column(weight, by_low)
            if x < last_x:
                state_next = (p_ref[x + 1, here, :], w_ref[x + 1, here, :], g_ref[x + 1, here, :])
                own_next = mobility_set(*state_next)
                flags = [u_ref[0, a, x + 1, here, :] > 0 for a in range(3)]
                x_face = face(own, own_next, t_ref[0, x + 1, here, :], flags, head_flat)
                flux, by_low, by_high = x_face
                res = [a + b for a, b in zip(res, flux)]
                diag = [a + b for a, b in zip(diag, by_low)]
                put(o_up, 0, by_high, 1)
                cols[4] = column(weight, by_high)

            shifted = []
            for k, ref in enumerate((p_ref, w_ref, g_ref)):
                entering = jnp.where(bottom, edge[k, x : x + 1, :], ref[x, pl.ds(before, 1), :])
                shifted.append(jnp.where(first_row, jnp.broadcast_to(entering, (size, lanes)), pltpu.roll(state[k], 1, 0)))
            flags = [u_ref[1, a, x, here, :] > 0 for a in range(3)]
            trans = jnp.where(live_y, t_ref[1, x, here, :], 0.0)
            flux, by_low, by_high = face(mobility_set(*shifted), own, trans, flags, head_flat)
            for k, value in enumerate(flux + by_low + by_high):
                fy[x, k, 0:size, :] = value
            res = [a - b for a, b in zip(res, flux)]
            diag = [a - b for a, b in zip(diag, by_high)]
            put(o_low, 1, by_low, -1)
            cols[2] = -column(weight, by_low)
            lifted = [fy[x, k, 1 : size + 1, :] for k in range(3 + 2 * distinct)]
            for k, value in enumerate(flux + by_low + by_high):
                fy[x, k, size : size + 1, :] = value[0:1]
            flux, by_low, by_high = lifted[:3], lifted[3 : 3 + distinct], lifted[3 + distinct :]
            res = [a + b for a, b in zip(res, flux)]
            diag = [a + b for a, b in zip(diag, by_low)]
            put(o_up, 1, by_high, 1)
            cols[5] = column(weight, by_high)

            shifted = [pltpu.roll(value, 1, 1) for value in state]
            flags = [u_ref[2, a, x, here, :] > 0 for a in range(3)]
            trans = jnp.where(lane > 0, t_ref[2, x, here, :], 0.0)
            flux, by_low, by_high = face(mobility_set(*shifted), own, trans, flags, head_depth)
            res = [a - b for a, b in zip(res, flux)]
            diag = [a - b for a, b in zip(diag, by_high)]
            put(o_low, 2, by_low, -1)
            cols[3] = -column(weight, by_low)
            flux, by_low, by_high = ([pltpu.roll(v, lanes - 1, 1) for v in group] for group in (flux, by_low, by_high))
            res = [a + b for a, b in zip(res, flux)]
            diag = [a + b for a, b in zip(diag, by_low)]
            put(o_up, 2, by_high, 1)
            cols[6] = column(weight, by_high)

            if x == 0 or x == last_x:
                side = 0 if x == 0 else 1
                known = [cols[4 if x == 0 else 1], cols[2], cols[3], cols[5], cols[6]]
                for k, value in enumerate(res + diag + known + [accum]):
                    part[side, k, here, :] = value
                continue
            cols[0] = column(weight, diag)
            for k in range(3):
                o_res[k, x, here, :] = res[k]
            for k in range(9):
                o_diag[k, x, here, :] = zero if entry_of[k] < 0 else diag[entry_of[k]]
            weights = prolong_of(cols, accum, x % 2 == 1, row_odd)
            for k in range(7):
                o_rows[k, x, here, :] = cols[k]
                o_pro[k, x, here, :] = weights[k]
            reduced = weight[0] * res[0] + weight[1] * res[1] + weight[2] * res[2]
            near, near_y = shares_of(weights, reduced, lanes)
            half = x // 2
            if x % 2 == 1:
                coarse[half, here, :] = near
                coarse_y[half, here, :] = near_y
                across = weights[4] * reduced
            else:
                coarse[half, here, :] = near + across
                coarse_y[half, here, :] = near_y
                coarse[half - 1, here, :] = coarse[half - 1, here, :] + weights[1] * reduced

        def send(k, src, dst):
            pltpu.make_async_copy(src, dst, sem.at[k, c]).start()

        for k, (src, dst) in enumerate(pieces(here)):
            send(k, src, dst)
        return carry

    def pieces(here):
        inner = pl.ds(1, span_x - 2)
        return [
            (o_res.at[:, inner, here], res_hbm.at[:, inner, here]),
            (o_diag.at[:, inner, here], diag_hbm.at[:, inner, here]),
            (o_rows.at[:, inner, here], rows_hbm.at[:, inner, here]),
            (o_pro.at[:, inner, here], pro_hbm.at[:, inner, here]),
            (o_low.at[0, :, pl.ds(1, span_x - 1), here], low_hbm.at[0, :, pl.ds(1, span_x - 1), here]),
            (o_up.at[0, :, pl.ds(0, span_x - 1), here], up_hbm.at[0, :, pl.ds(0, span_x - 1), here]),
            (o_low.at[pl.ds(1, 2), :, :, here], low_hbm.at[pl.ds(1, 2), :, :, here]),
            (o_up.at[pl.ds(1, 2), :, :, here], up_hbm.at[pl.ds(1, 2), :, :, here]),
        ]

    lax.fori_loop(0, chunks, chunk, 0)

    def drain(c, carry):
        here = pl.ds(pl.multiple_of(c * size, size), size)
        for k, (src, dst) in enumerate(pieces(here)):
            pltpu.make_async_copy(src, dst, sem.at[k, c]).wait()
        return carry

    lax.fori_loop(0, chunks, drain, 0)


def edge_kernel(
    part, mine_up, mine_dn, halo_lo, halo_hi, coarse_in, coarse_y_in,
    res_in, diag_in, low_in, up_in, rows_in, pro_in,
    res_hbm, diag_hbm, low_hbm, up_hbm, rows_hbm, pro_hbm, coarse, xev, xod, yev, yod,
    o_res, o_diag, o_blk, o_rows, o_pro, grid, grid_y, across, sem,
):
    span_y, lanes = mine_up.shape[1:]
    last_x = res_hbm.shape[1] - 1
    size = 8
    chunks = span_y // size
    pad = size
    row = lax.broadcasted_iota(jnp.int32, (size, lanes), 0)
    row_odd = row % 2 == 1
    zero = jnp.zeros((size, lanes), f32)
    for half in range(2):
        grid_y[half, 0:pad, :] = zero
        grid_y[half, pad + span_y : pad + span_y + pad, :] = zero

    def chunk(c, carry):
        base = pl.multiple_of(c * size, size)
        here = pl.ds(base, size)
        for side in range(2):
            res = [part[side, k, here, :] for k in range(3)]
            diag = [part[side, 3 + k, here, :] for k in range(distinct)]
            known = [part[side, 10 + k, here, :] for k in range(5)]
            accum = part[side, 15, here, :]
            cols = [None, known[0], known[1], known[2], known[0], known[3], known[4]]
            if side == 0:
                low = [halo_lo[k, here, :] for k in range(3)]
                high = [mine_dn[k, here, :] for k in range(7)]
            else:
                low = [mine_up[k, here, :] for k in range(3)]
                high = [halo_hi[k, here, :] for k in range(7)]
            flags = [a > 0.5 for a in high[4:]]
            flux, by_low, by_high = face(mobility_set(*low), mobility_set(*high[:3]), high[3], flags, head_flat)
            if side == 0:
                weight = weights_of(high[0])
                res = [a - b for a, b in zip(res, flux)]
                diag = [a - b for a, b in zip(diag, by_high)]
                block = [-v for v in by_low]
                cols[1] = column(weight, block)
            else:
                weight = weights_of(low[0])
                res = [a + b for a, b in zip(res, flux)]
                diag = [a + b for a, b in zip(diag, by_low)]
                block = by_high
                cols[4] = column(weight, block)
            cols[0] = column(weight, diag)
            for k in range(3):
                o_res[side, k, here, :] = res[k]
            for k in range(9):
                o_diag[side, k, here, :] = zero if entry_of[k] < 0 else diag[entry_of[k]]
                o_blk[side, k, here, :] = zero if entry_of[k] < 0 else block[entry_of[k]]
            weights = prolong_of(cols, accum, side == 1, row_odd)
            for k in range(7):
                o_rows[side, k, here, :] = cols[k]
                o_pro[side, k, here, :] = weights[k]
            reduced = weight[0] * res[0] + weight[1] * res[1] + weight[2] * res[2]
            near, near_y = shares_of(weights, reduced, lanes)
            grid[side, here, :] = coarse_in[side, here, :] + near
            grid_y[side, pl.ds(base + pad, size), :] = coarse_y_in[side, here, :] + near_y
            across[side, here, :] = weights[1 if side == 0 else 4] * reduced
        return carry

    lax.fori_loop(0, chunks, chunk, 0)
    copies = []

    def send(src, dst):
        copy = pltpu.make_async_copy(src, dst, sem.at[len(copies)])
        copy.start()
        copies.append(copy)

    for side, x in ((0, 0), (1, last_x)):
        send(o_res.at[side], res_hbm.at[:, x])
        send(o_diag.at[side], diag_hbm.at[:, x])
        send(o_blk.at[side], low_hbm.at[0, :, x] if side == 0 else up_hbm.at[0, :, x])
        send(o_rows.at[side], rows_hbm.at[:, x])
        send(o_pro.at[side], pro_hbm.at[:, x])
    half_y = span_y // 2
    gx_even = lax.axis_index("gx") % 2 == 0
    gy_even = lax.axis_index("gy") % 2 == 0
    down = across[0, pl.ds(0, half_y, 2), :] + across[0, pl.ds(1, half_y, 2), :]
    up = across[1, pl.ds(0, half_y, 2), :] + across[1, pl.ds(1, half_y, 2), :]
    xev[...] = jnp.where(gx_even, up, down)
    xod[...] = jnp.where(gx_even, down, up)
    for half in range(2):
        coarse[half] = (
            grid[half, pl.ds(0, half_y, 2), :]
            + grid[half, pl.ds(1, half_y, 2), :]
            + grid_y[half, pl.ds(pad + 2, half_y, 2), :]
            + grid_y[half, pl.ds(pad - 1, half_y, 2), :]
        )
        down = grid_y[half, pad : pad + 1, :]
        up = grid_y[half, pad + span_y - 1 : pad + span_y, :]
        yev[half : half + 1, :] = jnp.where(gy_even, up, down)
        yod[half : half + 1, :] = jnp.where(gy_even, down, up)
    for copy in copies:
        copy.wait()


def last_kernel(coarse, xev, xod, yev, yod, out):
    half_y = coarse.shape[1]
    gx_even = lax.axis_index("gx") % 2 == 0
    gy_even = lax.axis_index("gy") % 2 == 0
    out[0] = coarse[0] + jnp.where(gx_even, xod[...], xev[...])
    out[1] = coarse[1] + jnp.where(gx_even, xev[...], xod[...])
    low = jnp.where(gy_even, yod[...], yev[...])
    high = jnp.where(gy_even, yev[...], yod[...])
    for half in range(2):
        out[half, 0:1, :] = out[half, 0:1, :] + low[half : half + 1]
        out[half, half_y - 1 : half_y, :] = out[half, half_y - 1 : half_y, :] + high[half : half + 1]


def ring_of(axis, steps):
    count = lax.axis_size(axis)
    return [(i, (i + steps) % count) for i in range(count)]


def swap_of(axis, start):
    count = lax.axis_size(axis)
    pairs = []
    for i in range(start, count + start, 2):
        a, b = i % count, (i + 1) % count
        pairs += [(a, b), (b, a)]
    return pairs


hbm = pl.BlockSpec(memory_space=pl.ANY)
vmem = pl.BlockSpec(memory_space=pltpu.VMEM)


def shape_of(*shape):
    return jax.ShapeDtypeStruct(shape, f32)


def body(pressure, sat_water, sat_gas, pore_volume, mass_old, transmissibility, upwind):
    sx, sy, sz = pressure.shape
    xup, xdn, yev, yod = pl.pallas_call(
        pack_kernel,
        out_shape=[shape_of(3, sy, sz), shape_of(7, sy, sz), shape_of(7, sx, sz), shape_of(7, sx, sz)],
        in_specs=[hbm] * 5,
        out_specs=[vmem] * 4,
        scratch_shapes=[
            pltpu.VMEM((3, sx, 8, sz), f32),
            pltpu.VMEM((3, sx, 8, sz), f32),
            pltpu.VMEM((sx, 8, sz), f32),
            pltpu.VMEM((3, sx, 8, sz), jnp.int32),
            pltpu.VMEM((3, sy, sz), jnp.int32),
            pltpu.SemaphoreType.DMA((16,)),
        ],
        name="pack",
    )(pressure, sat_water, sat_gas, transmissibility, upwind)
    yev_in = lax.ppermute(yev, "gy", swap_of("gy", 0))
    yod_in = lax.ppermute(yod, "gy", swap_of("gy", 1))
    halo_hi = lax.ppermute(xdn, "gx", ring_of("gx", -1))
    halo_lo = lax.ppermute(xup, "gx", ring_of("gx", 1))
    outs = pl.pallas_call(
        main_kernel,
        out_shape=[
            shape_of(3, sx, sy, sz),
            shape_of(9, sx, sy, sz),
            shape_of(3, 9, sx, sy, sz),
            shape_of(3, 9, sx, sy, sz),
            shape_of(7, sx, sy, sz),
            shape_of(7, sx, sy, sz),
            shape_of(2, 16, sy, sz),
            shape_of(2, sy, sz),
            shape_of(2, sy, sz),
        ],
        in_specs=[vmem] * 9,
        out_specs=[hbm] * 6 + [vmem] * 3,
        scratch_shapes=[
            pltpu.VMEM((3, sx, sy, sz), f32),
            pltpu.VMEM((9, sx, sy, sz), f32),
            pltpu.VMEM((3, 9, sx, sy, sz), f32),
            pltpu.VMEM((3, 9, sx, sy, sz), f32),
            pltpu.VMEM((7, sx, sy, sz), f32),
            pltpu.VMEM((7, sx, sy, sz), f32),
            pltpu.VMEM((sx, 17, 16, sz), f32),
            pltpu.VMEM((3, sx, sz), f32),
            pltpu.SemaphoreType.DMA((8, sy // 8)),
        ],
        name="cells",
    )(pressure, sat_water, sat_gas, pore_volume, mass_old, transmissibility, upwind, yev_in, yod_in)
    big, (part, coarse, coarse_y) = outs[:6], outs[6:]
    outs = pl.pallas_call(
        edge_kernel,
        out_shape=[shape_of(*value.shape) for value in big]
        + [shape_of(2, sy // 2, sz), shape_of(sy // 2, sz), shape_of(sy // 2, sz), shape_of(2, sz), shape_of(2, sz)],
        in_specs=[vmem] * 7 + [hbm] * 6,
        out_specs=[hbm] * 6 + [vmem] * 5,
        input_output_aliases={7 + k: k for k in range(6)},
        scratch_shapes=[
            pltpu.VMEM((2, 3, sy, sz), f32),
            pltpu.VMEM((2, 9, sy, sz), f32),
            pltpu.VMEM((2, 9, sy, sz), f32),
            pltpu.VMEM((2, 7, sy, sz), f32),
            pltpu.VMEM((2, 7, sy, sz), f32),
            pltpu.VMEM((2, sy, sz), f32),
            pltpu.VMEM((2, sy + 16, sz), f32),
            pltpu.VMEM((2, sy, sz), f32),
            pltpu.SemaphoreType.DMA((10,)),
        ],
        name="edges",
    )(part, xup, xdn, halo_lo, halo_hi, coarse, coarse_y, *big)
    big, (coarse, xev, xod, yev, yod) = outs[:6], outs[6:]
    xev = lax.ppermute(xev, "gx", swap_of("gx", 0))
    xod = lax.ppermute(xod, "gx", swap_of("gx", 1))
    yev = lax.ppermute(yev, "gy", swap_of("gy", 0))
    yod = lax.ppermute(yod, "gy", swap_of("gy", 1))
    coarse = pl.pallas_call(
        last_kernel,
        out_shape=shape_of(2, sy // 2, sz),
        in_specs=[vmem] * 5,
        out_specs=vmem,
        name="finish",
    )(coarse, xev, xod, yev, yod)
    return (*big, coarse)


def solution(mesh):
    in_specs = (
        P("gx", "gy", None),
        P("gx", "gy", None),
        P("gx", "gy", None),
        P("gx", "gy", None),
        P(None, "gx", "gy", None),
        P(None, "gx", "gy", None),
        P(None, None, "gx", "gy", None),
    )
    out_specs = (
        P(None, "gx", "gy", None),
        P(None, "gx", "gy", None),
        P(None, None, "gx", "gy", None),
        P(None, None, "gx", "gy", None),
        P(None, "gx", "gy", None),
        P(None, "gx", "gy", None),
        P("gx", "gy", None),
    )
    return jax.shard_map(body, mesh=mesh, in_specs=in_specs, out_specs=out_specs, check_vma=False)
```

time: 80.7 us -> 45.2 us (0.56)
  the two profiles are of different devices: /device:TPU:129 before, /device:TPU:1 now
where the time goes in v1:
time: 45.2 us; the launch traced here: 45 us
  starting transfers between devices  21.8 us (48%)
  Pallas kernels  15.4 us (34%)
  waiting for transfers between devices  5.14 us (11%)
  local copies, waits for them, and re-layouts  1.92 us (4%)
  between operations  0.73 us (2%)
    ppermute x1, starting transfers between devices, body(): halo_hi = lax.ppermute(xdn, 'gx', ring_of('gx', -1))  11.4 us
    ppermute x1, starting transfers between devices, body(): xod = lax.ppermute(xod, 'gx', swap_of('gx', 1))  7.75 us
    pallas_call x1, Pallas kernels, body(): pl.pallas_call(main_kernel, out_shape=[shape_of(3, sx, sy, sz), shape_of(...  7.34 us
    pallas_call x1, Pallas kernels, body(): pl.pallas_call(edge_kernel, out_shape=[shape_of(*value.shape) for value i...  4.66 us
    ppermute x1, waiting for transfers between devices, body(): yod_in = lax.ppermute(yod, 'gy', swap_of('gy', 1))  2.4 us
    pallas_call x1, Pallas kernels, body(): pl.pallas_call(pack_kernel, out_shape=[shape_of(3, sy, sz), shape_of(7, s...  1.97 us
    unnamed x16, local copies, waits for them, and re-layouts  1.92 us
    ppermute x1, waiting for transfers between devices, body(): yod = lax.ppermute(yod, 'gy', swap_of('gy', 1))  1.88 us
  transfers between devices with their start and end apart: 8, of which 3 were waited for; matrix products, arithmetic and copies ran while one was open for 0% of the time, Pallas kernels for 16%

profile of v1, /device:TPU:1, one launch (start us, length us, event | category | flops | bytes accessed | tf_op | source)
XLA Modules:
  0.0 45.0 jit_solution(1118311352206273977)
XLA Ops:
  0.6 2.0 %pack.1 = (f32[3,64,128]{2,1,0:T(8,128)}, f32[7,64,128]{2,1,0:T(8,128)}, f32[7,4,128]{2,1,0:T(4,128)}, f32[7,4,128]{2,1,0:T(4,128)}) custom-call(f32[4,64,128]{2,1,0:T(8,128)} %p_ref.1, f32[4,64,128]{2,1,0:T(8,128)} %w_ref.1, f32[4,64,128]{2,1,0:T(8,128)} %g_ref.1, f32[3,4,64,128]{3,2,1,0:T(8,128)} %t_ref.1, s32[3,3,4,64,128]{4,3,2,1,0:T(8,128)} %u_ref.1), custom_call_target="tpu_custom_call" | custom-call | tf_op jit(solution)/shard_map/pack/pallas_call | solution.py:475
  2.6 11.4 %collective-permute-start.3 = (f32[7,64,128]{2,1,0:T(8,128)}, f32[7,64,128]{2,1,0:T(8,128)S(1)}, u32[]{:S(2)}, u32[]{:S(2)}) collective-permute-start(f32[7,64,128]{2,1,0:T(8,128)} %get-tuple-element.35.mine_dn), channel_id=1, source_target_pairs={{0,252},{4,0},{8,4},{12,8},{16,12},{20,16},{24,20},{28,24},{32,28}... | collective-permute-start | bytes 688136 | tf_op jit(solution)/shard_map/ppermute | solution.py:492
  14.0 0.0 collective-permute-start.2
  14.0 1.0 %collective-permute-start = (f32[7,4,128]{2,1,0:T(4,128)}, f32[7,4,128]{2,1,0:T(4,128)S(1)}, u32[]{:S(2)}, u32[]{:S(2)}) collective-permute-start(f32[7,4,128]{2,1,0:T(4,128)} %get-tuple-element.31), channel_id=1, source_target_pairs={{0,1},{1,0},{2,3},{3,2},{4,5},{5,4},{6,7},{7,6},{8,9},{9,8},{10,11... | collective-permute-start | bytes 43016 | tf_op jit(solution)/shard_map/ppermute | solution.py:490
  14.9 0.2 collective-permute-start.1
  15.1 0.8 %collective-permute-done.yev = f32[7,4,128]{2,1,0:T(4,128)S(1)} collective-permute-done((f32[7,4,128]{2,1,0:T(4,128)}, f32[7,4,128]{2,1,0:T(4,128)S(1)}, u32[]{:S(2)}, u32[]{:S(2)}) %collective-permute-start) | collective-permute-done | bytes 14368 | tf_op jit(solution)/shard_map/ppermute | solution.py:490
  16.0 2.4 %collective-permute-done.1.yod = f32[7,4,128]{2,1,0:T(4,128)S(1)} collective-permute-done((f32[7,4,128]{2,1,0:T(4,128)}, f32[7,4,128]{2,1,0:T(4,128)S(1)}, u32[]{:S(2)}, u32[]{:S(2)}) %collective-permute-start.1) | collective-permute-done | bytes 14368 | tf_op jit(solution)/shard_map/ppermute | solution.py:491
  18.4 0.6 %copy-done.5 = f32[7,4,128]{2,1,0:T(4,128)} copy-done((f32[7,4,128]{2,1,0:T(4,128)}, f32[7,4,128]{2,1,0:T(4,128)S(1)}, u32[]{:S(2)}) %copy-start.5) | copy-done | bytes 14360
  19.0 7.3 %cells.1 = (f32[3,4,64,128]{3,2,1,0:T(8,128)}, f32[9,4,64,128]{3,2,1,0:T(8,128)}, f32[3,9,4,64,128]{4,3,2,1,0:T(8,128)}, f32[3,9,4,64,128]{4,3,2,1,0:T(8,128)}, ...) custom-call(f32[4,64,128]{2,1,0:T(8,128)} %p_ref.1, ...), custom_call_target="tpu_custom_call" | custom-call | tf_op jit(solution)/shard_map/cells/pallas_call | solution.py:494
  26.4 0.6 %copy-done.1 = f32[3,64,128]{2,1,0:T(8,128)} copy-done((f32[3,64,128]{2,1,0:T(8,128)}, f32[3,64,128]{2,1,0:T(8,128)S(1)}, u32[]{:S(2)}) %copy-start.1) | copy-done | bytes 98328
  27.0 0.1 copy-done
  27.1 4.7 %edges.1 = (f32[3,4,64,128]{3,2,1,0:T(8,128)}, f32[9,4,64,128]{3,2,1,0:T(8,128)}, f32[3,9,4,64,128]{4,3,2,1,0:T(8,128)}, f32[3,9,4,64,128]{4,3,2,1,0:T(8,128)}, ...) custom-call(f32[2,16,64,128]{3,2,1,0:T(8,128)} %get-tuple-element.33, ...), custom_call_target="tpu_custom_call", output_to_operand_aliasing={{0}: (7, {}), {1}: (8, {}), {2}: (9, {}), {3}: (10, {}), {4... | custom-call | tf_op jit(solution)/shard_map/edges/pallas_call | solution.py:523
  31.8 0.1 collective-permute-start.4
  31.9 7.8 %collective-permute-start.5 = (f32[32,128]{1,0:T(8,128)}, f32[32,128]{1,0:T(8,128)S(1)}, u32[]{:S(2)}, u32[]{:S(2)}) collective-permute-start(f32[32,128]{1,0:T(8,128)} %get-tuple-element.52), channel_id=1, source_target_pairs={{4,8},{8,4},{12,16},{16,12},{20,24},{24,20},{28,32},{32,28},{36,40... | collective-permute-start | bytes 49160 | tf_op jit(solution)/shard_map/ppermute | solution.py:545
  39.6 0.0 collective-permute-start.6
  39.6 1.4 %collective-permute-start.7 = (f32[2,128]{1,0:T(2,128)}, f32[2,128]{1,0:T(2,128)S(1)}, u32[]{:S(2)}, u32[]{:S(2)}) collective-permute-start(f32[2,128]{1,0:T(2,128)} %get-tuple-element.54), channel_id=1, source_target_pairs={{1,2},{2,1},{3,0},{0,3},{5,6},{6,5},{7,4},{4,7},{9,10},{10,9},{11,... | collective-permute-start | bytes 3080 | tf_op jit(solution)/shard_map/ppermute | solution.py:547
  41.1 0.0 collective-permute-done.6.yev
  41.1 1.9 %collective-permute-done.7.yod = f32[2,128]{1,0:T(2,128)S(1)} collective-permute-done((f32[2,128]{1,0:T(2,128)}, f32[2,128]{1,0:T(2,128)S(1)}, u32[]{:S(2)}, u32[]{:S(2)}) %collective-permute-start.7) | collective-permute-done | bytes 1056 | tf_op jit(solution)/shard_map/ppermute | solution.py:547
  43.0 0.0 collective-permute-done.4.xev
  43.0 0.0 collective-permute-done.5.xod
  43.0 0.5 %copy-done.7 = f32[2,128]{1,0:T(2,128)} copy-done((f32[2,128]{1,0:T(2,128)}, f32[2,128]{1,0:T(2,128)S(1)}, u32[]{:S(2)}) %copy-start.7) | copy-done | bytes 1048
  43.5 0.1 copy-done.2
  43.6 0.0 copy-done.3
  43.6 1.4 %finish.1 = f32[2,32,128]{2,1,0:T(8,128)} custom-call(f32[2,32,128]{2,1,0:T(8,128)} %get-tuple-element.50.coarse, f32[32,128]{1,0:T(8,128)} %copy-done.2, f32[32,128]{1,0:T(8,128)} %copy-done.3, f32[2,128]{1,0:T(2,128)} %copy-done.6, f32[2,128]{1,0:T(2,128)} %copy-done.7), custom_call_target="tpu_custom_call" | custom-call | tf_op jit(solution)/shard_map/finish/pallas_call | solution.py:548
  (12 shorter events, 0.0 us)
Async XLA Ops:
  2.6 23.8 %collective-permute-start.3 = (f32[7,64,128]{2,1,0:T(8,128)}, f32[7,64,128]{2,1,0:T(8,128)S(1)}, u32[]{:S(2)}, u32[]{:S(2)}) collective-permute-start(f32[7,64,128]{2,1,0:T(8,128)} %get-tuple-element.35.mine_dn), channel_id=1, source_target_pairs={{0,252},{4,0},{8,4},{12,8},{16,12},{20,16},{24,20},{28,24},{32,28}... | collective-permute-start | bytes 688136 | tf_op jit(solution)/shard_map/ppermute | solution.py:492
  14.0 12.4 %collective-permute-start.2 = (f32[3,64,128]{2,1,0:T(8,128)}, f32[3,64,128]{2,1,0:T(8,128)S(1)}, u32[]{:S(2)}, u32[]{:S(2)}) collective-permute-start(f32[3,64,128]{2,1,0:T(8,128)} %get-tuple-element.34.mine_up), channel_id=1, source_target_pairs={{0,4},{4,8},{8,12},{12,16},{16,20},{20,24},{24,28},{28,32},{32,36}... | collective-permute-start | bytes 294920 | tf_op jit(solution)/shard_map/ppermute | solution.py:493
  14.0 2.0 %collective-permute-start = (f32[7,4,128]{2,1,0:T(4,128)}, f32[7,4,128]{2,1,0:T(4,128)S(1)}, u32[]{:S(2)}, u32[]{:S(2)}) collective-permute-start(f32[7,4,128]{2,1,0:T(4,128)} %get-tuple-element.31), channel_id=1, source_target_pairs={{0,1},{1,0},{2,3},{3,2},{4,5},{5,4},{6,7},{7,6},{8,9},{9,8},{10,11... | collective-permute-start | bytes 43016 | tf_op jit(solution)/shard_map/ppermute | solution.py:490
  14.9 3.4 %collective-permute-start.1 = (f32[7,4,128]{2,1,0:T(4,128)}, f32[7,4,128]{2,1,0:T(4,128)S(1)}, u32[]{:S(2)}, u32[]{:S(2)}) collective-permute-start(f32[7,4,128]{2,1,0:T(4,128)} %get-tuple-element.32), channel_id=1, source_target_pairs={{1,2},{2,1},{3,0},{0,3},{5,6},{6,5},{7,4},{4,7},{9,10},{10,9},{11,... | collective-permute-start | bytes 43016 | tf_op jit(solution)/shard_map/ppermute | solution.py:491
  16.0 2.4 %copy-start.4 = (f32[7,4,128]{2,1,0:T(4,128)}, f32[7,4,128]{2,1,0:T(4,128)S(1)}, u32[]{:S(2)}) copy-start(f32[7,4,128]{2,1,0:T(4,128)S(1)} %collective-permute-done.yev) | copy-start | bytes 43012
  18.4 0.6 %copy-start.5 = (f32[7,4,128]{2,1,0:T(4,128)}, f32[7,4,128]{2,1,0:T(4,128)S(1)}, u32[]{:S(2)}) copy-start(f32[7,4,128]{2,1,0:T(4,128)S(1)} %collective-permute-done.1.yod) | copy-start | bytes 43012
  26.4 0.6 %copy-start.1 = (f32[3,64,128]{2,1,0:T(8,128)}, f32[3,64,128]{2,1,0:T(8,128)S(1)}, u32[]{:S(2)}) copy-start(f32[3,64,128]{2,1,0:T(8,128)S(1)} %collective-permute-done.2.halo_lo) | copy-start | bytes 294916
  26.4 0.7 %copy-start = (f32[7,64,128]{2,1,0:T(8,128)}, f32[7,64,128]{2,1,0:T(8,128)S(1)}, u32[]{:S(2)}) copy-start(f32[7,64,128]{2,1,0:T(8,128)S(1)} %collective-permute-done.3.halo_hi) | copy-start | bytes 688132
  31.8 11.2 %collective-permute-start.4 = (f32[32,128]{1,0:T(8,128)}, f32[32,128]{1,0:T(8,128)S(1)}, u32[]{:S(2)}, u32[]{:S(2)}) collective-permute-start(f32[32,128]{1,0:T(8,128)} %get-tuple-element.51), channel_id=1, source_target_pairs={{0,4},{4,0},{8,12},{12,8},{16,20},{20,16},{24,28},{28,24},{32,36},... | collective-permute-start | bytes 49160 | tf_op jit(solution)/shard_map/ppermute | solution.py:544
  31.9 11.1 %collective-permute-start.5 = (f32[32,128]{1,0:T(8,128)}, f32[32,128]{1,0:T(8,128)S(1)}, u32[]{:S(2)}, u32[]{:S(2)}) collective-permute-start(f32[32,128]{1,0:T(8,128)} %get-tuple-element.52), channel_id=1, source_target_pairs={{4,8},{8,4},{12,16},{16,12},{20,24},{24,20},{28,32},{32,28},{36,40... | collective-permute-start | bytes 49160 | tf_op jit(solution)/shard_map/ppermute | solution.py:545
  39.6 1.4 %collective-permute-start.6 = (f32[2,128]{1,0:T(2,128)}, f32[2,128]{1,0:T(2,128)S(1)}, u32[]{:S(2)}, u32[]{:S(2)}) collective-permute-start(f32[2,128]{1,0:T(2,128)} %get-tuple-element.53), channel_id=1, source_target_pairs={{0,1},{1,0},{2,3},{3,2},{4,5},{5,4},{6,7},{7,6},{8,9},{9,8},{10,11... | collective-permute-start | bytes 3080 | tf_op jit(solution)/shard_map/ppermute | solution.py:546
  39.6 3.3 %collective-permute-start.7 = (f32[2,128]{1,0:T(2,128)}, f32[2,128]{1,0:T(2,128)S(1)}, u32[]{:S(2)}, u32[]{:S(2)}) collective-permute-start(f32[2,128]{1,0:T(2,128)} %get-tuple-element.54), channel_id=1, source_target_pairs={{1,2},{2,1},{3,0},{0,3},{5,6},{6,5},{7,4},{4,7},{9,10},{10,9},{11,... | collective-permute-start | bytes 3080 | tf_op jit(solution)/shard_map/ppermute | solution.py:547
  41.1 1.9 %copy-start.6 = (f32[2,128]{1,0:T(2,128)}, f32[2,128]{1,0:T(2,128)S(1)}, u32[]{:S(2)}) copy-start(f32[2,128]{1,0:T(2,128)S(1)} %collective-permute-done.6.yev) | copy-start | bytes 3076
  43.0 0.5 %copy-start.7 = (f32[2,128]{1,0:T(2,128)}, f32[2,128]{1,0:T(2,128)S(1)}, u32[]{:S(2)}) copy-start(f32[2,128]{1,0:T(2,128)S(1)} %collective-permute-done.7.yod) | copy-start | bytes 3076
  43.0 0.6 %copy-start.2 = (f32[32,128]{1,0:T(8,128)}, f32[32,128]{1,0:T(8,128)S(1)}, u32[]{:S(2)}) copy-start(f32[32,128]{1,0:T(8,128)S(1)} %collective-permute-done.4.xev) | copy-start | bytes 49156
  43.0 0.6 %copy-start.3 = (f32[32,128]{1,0:T(8,128)}, f32[32,128]{1,0:T(8,128)S(1)}, u32[]{:S(2)}) copy-start(f32[32,128]{1,0:T(8,128)S(1)} %collective-permute-done.5.xod) | copy-start | bytes 49156
